TPU v7x, 128 devices: a whole 4x4x4 slice. The times are simulated.
128 devices in a mesh: rows: 16 (over z_lo, x, core), cols: 8 (over z_hi, y).
Axes of the slice: x: 4, y: 4, z: 4 (z_hi: 2, z_lo: 2; z = z_hi * 2 + z_lo), core: 2. Of those that a mesh axis runs over, the one named last changes fastest.
Arguments:
- spectrum: bfloat16 [2, 4096, 4096], P(None, 'rows', 'cols'), may hold values from -6 to 6
- diffraction: bfloat16 [2, 32, 3, 128, 128], P(None, 'rows'), may hold values from -0.21875 to 0.21875
- order_mask: int32 [32, 3], P('rows'), may hold values from 0 to 1, as said below
- phases: float32 [2, 4096, 4096], P(None, 'rows', 'cols'), may hold values from -3.140625 to 3.140625
- transmission: float32 [4096, 4096], P('rows', 'cols'), may hold values from 0.2 to 1
- shifts: int32 [2], replicated, may hold values from 128 to 256, as said below
Outputs:
- outgoing: float32 [2, 4096, 4096], P(None, 'rows', 'cols')
Inputs may be any that keep to these rules, and one draw needn't show every extreme that they name: Each bounce's shift lies between 128 and 256; one bounce shifts by exactly 256. `order_mask`: every block carries the orders -1 and +1; the order 0 is off in some blocks.
All inputs are finite; a program needn't handle non-finite values.
Results may differ from a plain program's by a relative error of at most 0.018.
Values may be sent and summed in bfloat16 or wider, within the bound.
A program may use at most 128 MiB of HBM per device.

v0:
```python
import math
import jax
import jax.numpy as jnp
from jax import lax
from jax.sharding import PartitionSpec as P

BLOCK = 128
BASE = 256
BOUNCES = 2


def shifted(value, axis, steps):
    count = lax.axis_size(axis)
    first, last = (max(0, -steps), min(count, count - steps))
    return lax.ppermute(value, axis, [(source, source + steps) for source in range(first, last)])


def twiddles(extent, sign_value, left_index, right_index):
    wrapped = left_index[:, None] * right_index[None, :] % extent
    angles = wrapped.astype(jnp.float32) * (2.0 * math.pi / extent)
    return (jnp.cos(angles), sign_value * jnp.sin(angles))


def base_tables(target, extent, sign_value):
    turn_real, turn_imag = twiddles(extent, sign_value, jnp.arange(BASE, dtype=jnp.int32), target)
    factor = 1.0 / math.sqrt(extent)
    return ((turn_real * factor).astype(jnp.bfloat16), (turn_imag * factor).astype(jnp.bfloat16))


def blocked_dft(values, axis_at, sign_value, target, extent):
    block_count = values.shape[axis_at] // BASE
    base_real, base_imag = base_tables(target, extent, sign_value)
    if axis_at == 1:
        shaped = values.reshape(2, block_count, BASE, values.shape[2])
        form_text = "sio,ik->sko"
    else:
        shaped = values.reshape(2, values.shape[1], block_count, BASE)
        form_text = "osi,ik->sok"

    def contract(left_side, right_side):
        return jnp.einsum(form_text, left_side, right_side, preferred_element_type=jnp.float32)

    inner_real = contract(shaped[0], base_real) - contract(shaped[1], base_imag)
    inner_imag = contract(shaped[0], base_imag) + contract(shaped[1], base_real)
    numbers = jnp.arange(block_count, dtype=jnp.int32) * BASE
    turn_real, turn_imag = twiddles(extent, sign_value, numbers, target)
    if axis_at == 1:
        turn_real = turn_real[:, :, None]
        turn_imag = turn_imag[:, :, None]
    else:
        turn_real = turn_real[:, None, :]
        turn_imag = turn_imag[:, None, :]
    out_real = jnp.sum(turn_real * inner_real - turn_imag * inner_imag, axis=0)
    out_imag = jnp.sum(turn_real * inner_imag + turn_imag * inner_real, axis=0)
    return jnp.stack([out_real, out_imag])


def apply_blocks(left_side, right_side):
    return jnp.einsum("bjk,bkq->bjq", left_side, right_side, preferred_element_type=jnp.float32)


def diffract(current, offset_step, matrices, weights):
    below_rows = shifted(current, "rows", 1)
    above_rows = shifted(current, "rows", -1)
    widened = jnp.concatenate([below_rows, current, above_rows], axis=1)
    height = current.shape[1]
    columns = current.shape[2]
    block_count = height // BLOCK
    result_real = jnp.zeros((block_count, BLOCK, columns), jnp.float32)
    result_imag = jnp.zeros((block_count, BLOCK, columns), jnp.float32)
    for order_at in range(3):
        source = lax.dynamic_slice_in_dim(widened, height + (order_at - 1) * offset_step, height, 1)
        source = source.reshape(2, block_count, BLOCK, columns)
        kernel = matrices[:, :, order_at]
        weight_now = weights[:, order_at][:, None, None]
        result_real = result_real + weight_now * (
            apply_blocks(kernel[0], source[0]) - apply_blocks(kernel[1], source[1])
        )
        result_imag = result_imag + weight_now * (
            apply_blocks(kernel[0], source[1]) + apply_blocks(kernel[1], source[0])
        )
    return (result_real.reshape(height, columns), result_imag.reshape(height, columns))


def on_device(spectrum, diffraction, order_mask, phases, transmission, shifts):
    local_rows = spectrum.shape[1]
    local_cols = spectrum.shape[2]
    row_count = lax.axis_size("rows")
    col_count = lax.axis_size("cols")
    full_rows = local_rows * row_count
    full_cols = local_cols * col_count
    own_rows = lax.axis_index("rows") * local_rows + jnp.arange(local_rows, dtype=jnp.int32)
    own_cols = lax.axis_index("cols") * local_cols + jnp.arange(local_cols, dtype=jnp.int32)
    weights = order_mask.astype(jnp.float32)

    def rows_gather(values, sign_value):
        summed = blocked_dft(
            lax.all_gather(values, "rows", axis=1, tiled=True), 1, sign_value, own_rows, full_rows
        )
        return summed.astype(jnp.bfloat16)

    def columns_gather(values, sign_value):
        return blocked_dft(
            lax.all_gather(values, "cols", axis=2, tiled=True), 2, sign_value, own_cols, full_cols
        )

    current = spectrum
    outgoing = None
    for bounce in range(BOUNCES):
        closing = bounce == BOUNCES - 1
        diff_real, diff_imag = diffract(current, shifts[bounce], diffraction, weights)
        cosine = jnp.cos(phases[bounce])
        sine_part = jnp.sin(phases[bounce])
        wave_k = jnp.stack(
            [diff_real * cosine - diff_imag * sine_part, diff_real * sine_part + diff_imag * cosine]
        ).astype(jnp.bfloat16)
        rows_space = rows_gather(wave_k, 1.0)
        space = columns_gather(rows_space, 1.0) * transmission[None]
        if closing:
            outgoing = space
        else:
            columns_k = columns_gather(space.astype(jnp.bfloat16), -1.0).astype(jnp.bfloat16)
            current = rows_gather(columns_k, -1.0)
    return outgoing


def solution(mesh):
    placed = (
        P(None, "rows", "cols"),
        P(None, "rows", None, None, None),
        P("rows", None),
        P(None, "rows", "cols"),
        P("rows", "cols"),
        P(),
    )
    return jax.shard_map(
        on_device, mesh=mesh, in_specs=placed, out_specs=P(None, "rows", "cols"), check_vma=False
    )
```

profile of v0, /device:TPU:0, one launch (start us, length us, event | category | flops | bytes accessed | tf_op | source)
XLA Modules:
  0.0 625.4 jit_solution(12232110755991861289)
XLA Ops:
  6.5 1.4 collective-permute-start
  8.0 1.3 collective-permute-start.1
  9.3 1.1 fusion.321
  11.3 1.1 fusion.145
  12.3 1.1 fusion.46
  13.4 1.1 fusion.147
  14.5 1.4 fusion.322
  20.3 2.0 fusion.57
  22.3 0.8 pad_maximum_fusion.1
  24.1 58.0 %all-gather.7.cloned.1.call-done = bf16[2,4096,512]{2,1,0:T(8,128)(2,1)} async-done(((bf16[2,256,512]{2,1,0:T(8,128)(2,1)}), bf16[2,4096,512]{2,1,0:T(8,128)(2,1)}) %all-gather.7.cloned.1.call-update) | async-done | bytes 8388624 | tf_op jit(solution)/shard_map/all_gather | solution.py:98
  82.1 3.8 fusion.317
  85.8 2.2 fusion.109
  88.1 2.3 fusion.119
  90.3 2.2 fusion.111
  92.6 6.7 %fusion.21 = (bf16[256,512]{1,0:T(8,128)(2,1)S(1)}, bf16[256,512]{1,0:T(8,128)(2,1)S(1)}) fusion(f32[16,256]{1,0:T(8,128)S(1)} %get-tuple-element.50, f32[16,256]{1,0:T(8,128)S(1)} %get-tuple-element.51, f32[256,16,512]{2,0,1:T(8,128)S(1)} %fusion.109, f32[256,16,512]{2,0,1:T(8,128)S(1)} %fusion.111, f32[256,16,512]{2,0,1:T(8,128)S(1)} %fusion.119, ...), kind=kOutput, calls=%fused_computation.43 | convolution fusion | flops 1095499776 | bytes 29918208 | tf_op jit(solution)/shard_map/sio,ik->sko/dot_general | solution.py:41
  99.3 0.8 pad_maximum_fusion.2
  100.7 0.9 broadcast_multiply_fusion
  101.6 76.9 %all-gather.9.cloned.1.call-done = bf16[2,256,4096]{2,1,0:T(8,128)(2,1)} async-done(((bf16[2,256,512]{2,1,0:T(8,128)(2,1)}), bf16[2,256,4096]{2,1,0:T(8,128)(2,1)}) %all-gather.9.cloned.1.call-update) | async-done | bytes 4194320 | tf_op jit(solution)/shard_map/all_gather | solution.py:104
  178.4 4.7 fusion.320
  183.1 3.3 copy.41
  186.4 5.4 fusion.80
  191.8 5.4 fusion.90
  197.1 3.3 copy.39
  200.4 3.1 fusion.82
  203.8 10.2 %fusion.17 = (f32[256,512]{0,1:T(8,128)S(1)}, f32[256,512]{0,1:T(8,128)S(1)}) fusion(f32[16,512]{1,0:T(8,128)S(1)} %get-tuple-element.47, f32[16,512]{1,0:T(8,128)S(1)} %get-tuple-element.48, f32[512,256,16]{1,0,2:T(8,128)} %fusion.80, f32[512,256,16]{1,0,2:T(8,128)S(1)} %fusion.82, f32[512,256,16]{1,0,2:T(8,128)S(1)} %copy-done.1, ...), kind=kOutput, calls=%fused_computation.35 | convolution fusion | flops 1096548352 | bytes 28379136 | tf_op jit(solution)/shard_map/osi,ik->sok/dot_general | solution.py:41
  214.1 0.9 fusion.48
  215.5 69.9 %all-gather.11.cloned.1.call-done = bf16[2,256,4096]{1,2,0:T(8,128)(2,1)} async-done(((bf16[2,256,512]{1,2,0:T(8,128)(2,1)}), bf16[2,256,4096]{1,2,0:T(8,128)(2,1)}) %all-gather.11.cloned.1.call-update) | async-done | bytes 4194320 | tf_op jit(solution)/shard_map/all_gather | solution.py:104
  285.4 2.5 fusion.319
  287.9 3.1 fusion.76
  291.0 3.1 fusion.94
  294.2 3.1 fusion.78
  297.3 8.7 %fusion.13 = (bf16[256,512]{0,1:T(8,128)(2,1)S(1)}, bf16[256,512]{0,1:T(8,128)(2,1)S(1)}) fusion(f32[16,512]{1,0:T(8,128)S(1)} %get-tuple-element.46, f32[16,512]{1,0:T(8,128)S(1)} %get-tuple-element.48, f32[512,256,16]{1,0,2:T(8,128)S(1)} %fusion.76, f32[512,256,16]{1,0,2:T(8,128)S(1)} %fusion.78, f32[512,256,16]{1,0,2:T(8,128)S(1)} %fusion.94, ...), kind=kOutput, calls=%fused_computation.27 | convolution fusion | flops 1096548352 | bytes 27854848 | tf_op jit(solution)/shard_map/osi,ik->sok/dot_general | solution.py:41
  306.0 0.8 pad_maximum_fusion.3
  307.1 58.6 %all-gather.13.cloned.1.call-done = bf16[2,4096,512]{1,2,0:T(8,128)(2,1)} async-done(((bf16[2,256,512]{1,2,0:T(8,128)(2,1)}), bf16[2,4096,512]{1,2,0:T(8,128)(2,1)}) %all-gather.13.cloned.1.call-update) | async-done | bytes 8388624 | tf_op jit(solution)/shard_map/all_gather | solution.py:98
  365.8 6.0 fusion.316
  371.8 6.5 %copy.51 = bf16[1,4096,512]{2,1,0:T(8,128)(2,1)} copy(bf16[1,4096,512]{1,2,0:T(8,128)(2,1)} %get-tuple-element.22) | data formatting | bytes 8388608 | tf_op jit(solution)/shard_map/slice | solution.py:43
  378.2 7.8 %fusion.105 = f32[256,16,512]{2,0,1:T(8,128)} fusion(bf16[16,256,512]{2,1,0:T(8,128)(2,1)} %bitcast.390, s32[256]{0:T(256)S(1)} %copy-done.12), kind=kOutput, calls=%fused_computation.166 | convolution fusion | flops 1074790400 | bytes 12583936 | tf_op jit(solution)/shard_map/sio,ik->sko/dot_general | solution.py:41
  386.0 5.5 fusion.123
  391.5 6.5 %copy.50 = bf16[1,4096,512]{2,1,0:T(8,128)(2,1)} copy(bf16[1,4096,512]{1,2,0:T(8,128)(2,1)} %get-tuple-element.23) | data formatting | bytes 8388608 | tf_op jit(solution)/shard_map/slice | solution.py:43
  398.1 4.6 fusion.107
  402.7 1.3 copy-done.4
  404.0 8.0 %fusion.9 = (bf16[256,512]{1,0:T(8,128)(2,1)S(1)}, bf16[256,512]{1,0:T(8,128)(2,1)S(1)}) fusion(f32[16,256]{1,0:T(8,128)S(1)} %copy-done.15, f32[16,256]{1,0:T(8,128)S(1)} %get-tuple-element.51, f32[256,16,512]{2,0,1:T(8,128)} %fusion.105, f32[256,16,512]{2,0,1:T(8,128)S(1)} %fusion.107, f32[256,16,512]{2,0,1:T(8,128)S(1)} %copy-done.4, ...), kind=kOutput, calls=%fused_computation.19 | convolution fusion | flops 1095499776 | bytes 29918208 | tf_op jit(solution)/shard_map/sio,ik->sko/dot_general | solution.py:41
  412.0 1.3 collective-permute-start.3
  413.3 3.8 collective-permute-start.2
  419.5 0.8 copy-done.10
  420.3 1.3 pad_maximum_fusion
  424.2 2.1 fusion.53
  426.3 0.8 pad_maximum_fusion.5
  427.5 57.0 %all-gather.15.cloned.1.call-done = bf16[2,4096,512]{2,1,0:T(8,128)(2,1)} async-done(((bf16[2,256,512]{2,1,0:T(8,128)(2,1)}), bf16[2,4096,512]{2,1,0:T(8,128)(2,1)}) %all-gather.15.cloned.1.call-update) | async-done | bytes 8388624 | tf_op jit(solution)/shard_map/all_gather | solution.py:98
  484.4 3.8 fusion.315
  488.2 2.2 fusion.101
  490.5 2.3 fusion.115
  492.7 2.2 fusion.103
  495.0 6.7 %fusion.5 = (bf16[256,512]{1,0:T(8,128)(2,1)S(1)}, bf16[256,512]{1,0:T(8,128)(2,1)S(1)}) fusion(f32[16,256]{1,0:T(8,128)S(1)} %copy-done.14, f32[16,256]{1,0:T(8,128)S(1)} %get-tuple-element.51, f32[256,16,512]{2,0,1:T(8,128)S(1)} %fusion.101, f32[256,16,512]{2,0,1:T(8,128)S(1)} %fusion.103, f32[256,16,512]{2,0,1:T(8,128)S(1)} %fusion.115, ...), kind=kOutput, calls=%fused_computation.11 | convolution fusion | flops 1095499776 | bytes 29918208 | tf_op jit(solution)/shard_map/sio,ik->sko/dot_general | solution.py:41
  501.7 0.8 pad_maximum_fusion.6
  502.5 78.2 %all-gather.17.cloned.1.call-done = bf16[2,256,4096]{2,1,0:T(8,128)(2,1)} async-done(((bf16[2,256,512]{2,1,0:T(8,128)(2,1)}), bf16[2,256,4096]{2,1,0:T(8,128)(2,1)}) %all-gather.17.cloned.1.call-update) | async-done | bytes 4194320 | tf_op jit(solution)/shard_map/all_gather | solution.py:104
  580.8 4.7 fusion.318
  585.5 3.3 copy.54
  588.7 5.4 fusion.72
  594.1 5.4 fusion.86
  599.5 3.5 copy.52
  603.0 3.1 fusion.74
  606.4 10.2 %fusion.1 = (f32[256,512]{0,1:T(8,128)S(1)}, f32[256,512]{0,1:T(8,128)S(1)}) fusion(f32[16,512]{1,0:T(8,128)S(1)} %get-tuple-element.47, f32[16,512]{1,0:T(8,128)S(1)} %get-tuple-element.48, f32[512,256,16]{1,0,2:T(8,128)} %fusion.72, f32[512,256,16]{1,0,2:T(8,128)S(1)} %fusion.74, f32[512,256,16]{1,0,2:T(8,128)S(1)} %copy-done, ...), kind=kOutput, calls=%fused_computation.3 | convolution fusion | flops 1096548352 | bytes 28379136 | tf_op jit(solution)/shard_map/osi,ik->sok/dot_general | solution.py:41
  616.8 1.3 copy.58
  (95 shorter events, 9.1 us)
Async XLA Ops:
  6.5 11.6 %copy-start.6 = (bf16[2,256,512]{2,1,0:T(8,128)(2,1)S(1)}, bf16[2,256,512]{2,1,0:T(8,128)(2,1)}, u32[]{:S(2)}) copy-start(bf16[2,256,512]{2,1,0:T(8,128)(2,1)} %param.6) | copy-start | bytes 1572868
  6.5 11.3 %copy-start.5 = (bf16[2,2,3,128,128]{4,3,2,1,0:T(8,128)(2,1)S(1)}, bf16[2,2,3,128,128]{4,3,2,1,0:T(8,128)(2,1)}, u32[]{:S(2)}) copy-start(bf16[2,2,3,128,128]{4,3,2,1,0:T(8,128)(2,1)} %param.7) | copy-start | bytes 1179652
  6.5 75.5 %all-gather.7.cloned.1.call-start = ((), (), s32[]{:S(2)}) async-start(), calls=%async_computation | async-start | bytes 8912896 | tf_op jit(solution)/shard_map/all_gather | solution.py:98
  6.5 11.5 %collective-permute-start = (bf16[2,256,512]{2,1,0:T(8,128)(2,1)}, bf16[2,256,512]{2,1,0:T(8,128)(2,1)S(1)}, u32[]{:S(2)}, u32[]{:S(2)}) collective-permute-start(bf16[2,256,512]{2,1,0:T(8,128)(2,1)} %param.6), channel_id=1, source_target_pairs={{0,8},{8,16},{16,24},{24,32},{32,40},{40,48},{48,56},{56,64},{64,7... | collective-permute-start | bytes 1572872 | tf_op jit(solution)/shard_map/ppermute | solution.py:15
  8.0 10.2 %collective-permute-start.1 = (bf16[2,256,512]{2,1,0:T(8,128)(2,1)}, bf16[2,256,512]{2,1,0:T(8,128)(2,1)S(1)}, u32[]{:S(2)}, u32[]{:S(2)}) collective-permute-start(bf16[2,256,512]{2,1,0:T(8,128)(2,1)} %param.6), channel_id=1, source_target_pairs={{8,0},{16,8},{24,16},{32,24},{40,32},{48,40},{56,48},{64,56},{72,6... | collective-permute-start | bytes 1572872 | tf_op jit(solution)/shard_map/ppermute | solution.py:15
  11.3 7.2 %copy-start.16 = (f32[2]{0:T(128)}, f32[2]{0:T(128)S(1)}, u32[]{:S(2)}) copy-start(f32[2]{0:T(128)S(1)} %get-tuple-element.18) | copy-start | bytes 28
  11.3 8.3 %copy-start.18 = (f32[2]{0:T(128)}, f32[2]{0:T(128)S(1)}, u32[]{:S(2)}) copy-start(f32[2]{0:T(128)S(1)} %get-tuple-element.19) | copy-start | bytes 28
  11.3 8.8 %copy-start.20 = (f32[2]{0:T(128)}, f32[2]{0:T(128)S(1)}, u32[]{:S(2)}) copy-start(f32[2]{0:T(128)S(1)} %get-tuple-element.17) | copy-start | bytes 28
  19.1 1.2 copy-start.7
  23.2 155.2 %all-gather.9.cloned.1.call-start = ((), (), s32[]{:S(2)}) async-start(), calls=%async_computation.1 | async-start | bytes 4718592 | tf_op jit(solution)/shard_map/all_gather | solution.py:104
  23.3 62.6 %copy-start.22 = (s32[16]{0:T(128)}, s32[16]{0:T(128)S(1)}, u32[]{:S(2)}) copy-start(s32[16]{0:T(128)S(1)} %iota_multiply_fusion) | copy-start | bytes 196
  23.3 69.3 %copy-start.11 = (s32[256]{0:T(256)}, s32[256]{0:T(256)S(1)}, u32[]{:S(2)}) copy-start(s32[256]{0:T(256)S(1)} %iota_add_fusion.1) | copy-start | bytes 3076
  24.1 68.5 %copy-start.13 = (f32[16,256]{1,0:T(8,128)}, f32[16,256]{1,0:T(8,128)S(1)}, u32[]{:S(2)}) copy-start(f32[16,256]{1,0:T(8,128)S(1)} %get-tuple-element.50) | copy-start | bytes 49156
  92.6 7.9 %copy-start.9 = (f32[256,512]{1,0:T(8,128)S(1)}, f32[256,512]{1,0:T(8,128)}, u32[]{:S(2)}) copy-start(f32[256,512]{1,0:T(8,128)} %param.10) | copy-start | bytes 1572868
  100.2 185.2 %all-gather.11.cloned.1.call-start = ((), (), s32[]{:S(2)}) async-start(), calls=%async_computation.2 | async-start | bytes 4718592 | tf_op jit(solution)/shard_map/all_gather | solution.py:104
  200.4 3.4 copy-start.1
  215.0 150.8 %all-gather.13.cloned.1.call-start = ((), (), s32[]{:S(2)}) async-start(), calls=%async_computation.3 | async-start | bytes 8912896 | tf_op jit(solution)/shard_map/all_gather | solution.py:98
  306.9 177.5 %all-gather.15.cloned.1.call-start = ((), (), s32[]{:S(2)}) async-start(), calls=%async_computation.4 | async-start | bytes 8912896 | tf_op jit(solution)/shard_map/all_gather | solution.py:98
  371.8 6.5 %copy-start.12 = (s32[256]{0:T(256)S(1)}, s32[256]{0:T(256)}, u32[]{:S(2)}) copy-start(s32[256]{0:T(256)} %copy-done.11) | copy-start | bytes 3076
  378.2 7.8 %copy-start.2 = (bf16[1,4096,512]{2,1,0:T(8,128)(2,1)S(1)}, bf16[1,4096,512]{2,1,0:T(8,128)(2,1)}, u32[]{:S(2)}) copy-start(bf16[1,4096,512]{2,1,0:T(8,128)(2,1)} %copy.51) | copy-start | bytes 12582916
  391.5 11.1 %copy-start.15 = (f32[16,256]{1,0:T(8,128)S(1)}, f32[16,256]{1,0:T(8,128)}, u32[]{:S(2)}) copy-start(f32[16,256]{1,0:T(8,128)} %get-tuple-element.49) | copy-start | bytes 49156
  398.0 4.6 copy-start.3
  398.0 5.9 copy-start.4
  412.0 7.5 %collective-permute-start.3 = (bf16[2,256,512]{2,1,0:T(8,128)(2,1)S(1)}, bf16[2,256,512]{2,1,0:T(8,128)(2,1)S(1)}, u32[]{:S(2)}, u32[]{:S(2)}) collective-permute-start(bf16[2,256,512]{2,1,0:T(8,128)(2,1)S(1)} %pad_maximum_fusion.4), channel_id=1, source_target_pairs={{8,0},{16,8},{24,16},{32,24},{40,32},{48,40},{56,48},{64,56},{72,6... | collective-permute-start | bytes 1572872 | tf_op jit(solution)/shard_map/ppermute | solution.py:15
  413.3 7.0 %collective-permute-start.2 = (bf16[2,256,512]{2,1,0:T(8,128)(2,1)S(1)}, bf16[2,256,512]{2,1,0:T(8,128)(2,1)}, u32[]{:S(2)}, u32[]{:S(2)}) collective-permute-start(bf16[2,256,512]{2,1,0:T(8,128)(2,1)S(1)} %pad_maximum_fusion.4), channel_id=1, source_target_pairs={{0,8},{8,16},{16,24},{24,32},{32,40},{40,48},{48,56},{56,64},{64,7... | collective-permute-start | bytes 1572872 | tf_op jit(solution)/shard_map/ppermute | solution.py:15
  419.1 3.3 copy-start.19
  419.5 0.8 copy-start.10
  421.6 1.6 copy-start.17
  421.9 1.6 copy-start.21
  423.0 1.2 copy-start.8
  427.2 153.6 %all-gather.17.cloned.1.call-start = ((), (), s32[]{:S(2)}) async-start(), calls=%async_computation.5 | async-start | bytes 4718592 | tf_op jit(solution)/shard_map/all_gather | solution.py:104
  492.7 2.3 copy-start.14
  603.0 3.4 copy-start
Sparse Core Ops, SparseCore 0:
  23.3 58.6 all-gather.6
  100.3 78.0 all-gather.8
  215.1 70.2 all-gather.10
  307.0 58.6 all-gather.12
  427.3 57.0 all-gather.14
  502.7 78.0 all-gather.16
where the time goes:
time: 635 us; the launch traced here: 625 us
  waiting for transfers between devices  399 us (63%)
  matrix products  127 us (20%)
  local copies, waits for them, and re-layouts  59.3 us (9%)
  between operations  18.5 us (3%)
  other arithmetic  13 us (2%)
  starting transfers between devices  9.08 us (1%)
    all_gather x3, waiting for transfers between devices, columns_gather(): lax.all_gather(values, 'cols', axis=2, tiled=True)  225 us
    all_gather x3, waiting for transfers between devices, rows_gather(): lax.all_gather(values, 'rows', axis=1, tiled=True)  174 us
    dot_general x24, matrix products, contract(): jnp.einsum(form_text, left_side, right_side, preferred_element_type=jnp.f...  119 us
    slice x12, local copies, waits for them, and re-layouts, blocked_dft(): inner_real = contract(shaped[0], base_real) - contract(shaped[1], base_imag)  51.6 us
  transfers between devices with their start and end apart: 10, of which 6 were waited for; matrix products, arithmetic and copies ran while one was open for 1% of the time, Pallas kernels for 0%

commit v1 on v0

--- a/solution.py
+++ b/solution.py
@@ -101,7 +101,13 @@
 
     def columns_gather(values, sign_value):
         return blocked_dft(
-            lax.all_gather(values, "cols", axis=2, tiled=True), 2, sign_value, own_cols, full_cols
+            jnp.concatenate(
+                lax.all_to_all(jnp.stack([values] * lax.axis_size("cols")), "cols", 0, 0), axis=2
+            ),
+            2,
+            sign_value,
+            own_cols,
+            full_cols,
         )
 
     current = spectrum

time: 635 us -> 558 us (0.88)
  waiting for transfers between devices: 399 us -> 225 us
  blocking collectives: 0 us -> 126 us
  local copies, waits for them, and re-layouts: 59.3 us -> 40.5 us
  matrix products: 127 us -> 114 us
    all_gather x3 -> x0, waiting for transfers between devices: 225 us -> none  [columns_gather(): lax.all_gather(values, 'cols', axis=2, tiled=True)]
    all_to_all x0 -> x2, blocking collectives: none -> 126 us  [columns_gather(): lax.all_to_all(jnp.stack([values] * lax.axis_size('cols')), 'cols', 0, 0)]
    all_to_all x0 -> x1, waiting for transfers between devices: none -> 50.7 us  [columns_gather(): lax.all_to_all(jnp.stack([values] * lax.axis_size('cols')), 'cols', 0, 0)]
    slice x12 -> x8, local copies, waits for them, and re-layouts: 51.6 us -> 27.5 us  [blocked_dft(): inner_real = contract(shaped[0], base_real) - contract(shaped[1], base_imag)]
    dot_general x24, matrix products: 119 us -> 106 us  [contract(): jnp.einsum(form_text, left_side, right_side, preferred_element_type=jnp.f...]
    all_to_all x0 -> x1, starting transfers between devices: none -> 6.86 us  [columns_gather(): lax.all_to_all(jnp.stack([values] * lax.axis_size('cols')), 'cols', 0, 0)]
  transfers between devices with their start and end apart: 10 -> 8, of which waited for: 6 -> 4; matrix products, arithmetic and copies ran while one was open for 1% -> 1% of each run, Pallas kernels for 0% -> 0%
where the time goes in v1:
time: 558 us; the launch traced here: 548 us
  waiting for transfers between devices  225 us (40%)
  blocking collectives  126 us (23%)
  matrix products  114 us (20%)
  local copies, waits for them, and re-layouts  40.5 us (7%)
  between operations  18 us (3%)
  starting transfers between devices  15.4 us (3%)
  other arithmetic  9.43 us (2%)
    all_gather x3, waiting for transfers between devices, rows_gather(): lax.all_gather(values, 'rows', axis=1, tiled=True)  174 us
    all_to_all x2, blocking collectives, columns_gather(): lax.all_to_all(jnp.stack([values] * lax.axis_size('cols')), 'cols', 0, 0)  126 us
    dot_general x24, matrix products, contract(): jnp.einsum(form_text, left_side, right_side, preferred_element_type=jnp.f...  106 us
    all_to_all x1, waiting for transfers between devices, columns_gather(): lax.all_to_all(jnp.stack([values] * lax.axis_size('cols')), 'cols', 0, 0)  50.7 us
    slice x8, local copies, waits for them, and re-layouts, blocked_dft(): inner_real = contract(shaped[0], base_real) - contract(shaped[1], base_imag)  27.5 us
  transfers between devices with their start and end apart: 8, of which 4 were waited for; matrix products, arithmetic and copies ran while one was open for 1% of the time, Pallas kernels for 0%

profile of v1, /device:TPU:0, one launch (start us, length us, event | category | flops | bytes accessed | tf_op | source)
XLA Modules:
  0.0 548.4 jit_solution(13923018174712619399)
XLA Ops:
  6.5 1.4 collective-permute-start
  8.0 1.3 collective-permute-start.1
  9.3 1.1 fusion.321
  10.4 0.7 convert_element_type.88
  11.3 1.1 fusion.145
  12.3 1.1 fusion.46
  13.4 1.1 fusion.147
  14.4 1.3 fusion.322
  20.3 2.0 fusion.57
  22.3 0.8 pad_maximum_fusion.1
  23.3 58.7 %all-gather.4.cloned.1.call-done = bf16[2,4096,512]{2,1,0:T(8,128)(2,1)} async-done(((bf16[2,256,512]{2,1,0:T(8,128)(2,1)}), bf16[2,4096,512]{2,1,0:T(8,128)(2,1)}) %all-gather.4.cloned.1.call-update) | async-done | bytes 8388624 | tf_op jit(solution)/shard_map/all_gather | solution.py:98
  82.0 3.8 fusion.317
  85.8 2.2 fusion.109
  88.0 2.3 fusion.119
  90.3 2.2 fusion.111
  92.5 6.4 %fusion.21 = (bf16[256,512]{1,0:T(8,128)(2,1)S(1)}, bf16[256,512]{1,0:T(8,128)(2,1)S(1)}) fusion(f32[16,256]{1,0:T(8,128)S(1)} %get-tuple-element.50, f32[16,256]{1,0:T(8,128)S(1)} %get-tuple-element.51, f32[256,16,512]{2,0,1:T(8,128)S(1)} %fusion.109, f32[256,16,512]{2,0,1:T(8,128)S(1)} %fusion.111, f32[256,16,512]{2,0,1:T(8,128)S(1)} %fusion.119, ...), kind=kOutput, calls=%fused_computation.43 | convolution fusion | flops 1095499776 | bytes 29918208 | tf_op jit(solution)/shard_map/sio,ik->sko/dot_general | solution.py:41
  99.2 2.4 stack.109
  101.6 6.9 %all-to-all-start = ((bf16[8,2,256,512]{2,3,1,0:T(8,128)(2,1)}), bf16[8,2,256,512]{2,3,1,0:T(8,128)(2,1)}, u32[]{:S(2)}, u32[]{:S(2)}) async-start(bf16[8,2,256,512]{2,3,1,0:T(8,128)(2,1)} %stack.109), calls=%async_computation | async-start | bytes 8388608 | tf_op jit(solution)/shard_map/all_to_all | solution.py:105
  109.1 50.7 %all-to-all-done = bf16[8,2,256,512]{2,3,1,0:T(8,128)(2,1)} async-done(((bf16[8,2,256,512]{2,3,1,0:T(8,128)(2,1)}), bf16[8,2,256,512]{2,3,1,0:T(8,128)(2,1)}, u32[]{:S(2)}, u32[]{:S(2)}) %all-to-all-start) | async-done | bytes 4194336 | tf_op jit(solution)/shard_map/all_to_all | solution.py:105
  159.8 2.5 copy.82
  162.3 0.4 fusion.320
  162.6 3.1 fusion.80
  165.8 3.2 fusion.90
  168.9 3.1 fusion.82
  172.1 8.7 %fusion.17 = (f32[256,512]{0,1:T(8,128)S(1)}, f32[256,512]{0,1:T(8,128)S(1)}) fusion(f32[16,512]{1,0:T(8,128)S(1)} %get-tuple-element.47, f32[16,512]{1,0:T(8,128)S(1)} %get-tuple-element.48, f32[512,256,16]{1,0,2:T(8,128)S(1)} %fusion.80, f32[512,256,16]{1,0,2:T(8,128)S(1)} %fusion.82, f32[512,256,16]{1,0,2:T(8,128)S(1)} %fusion.90, ...), kind=kOutput, calls=%fused_computation.35 | convolution fusion | flops 1096548352 | bytes 28379136 | tf_op jit(solution)/shard_map/osi,ik->sok/dot_general | solution.py:41
  180.9 0.4 stack.113
  181.3 67.9 %all_to_all.15 = bf16[8,2,256,512]{2,3,1,0:T(8,128)(2,1)S(1)} all-to-all(bf16[8,2,256,512]{2,3,1,0:T(8,128)(2,1)S(1)} %stack.113), channel_id=1, replica_groups=mesh['rows'=16,'cols'=8] {'cols'}, dimensions={0} | all-to-all | bytes 8388608 | tf_op jit(solution)/shard_map/all_to_all | solution.py:105
  249.2 0.4 copy.81
  249.6 0.4 fusion.319
  250.0 3.1 fusion.76
  253.1 3.1 fusion.94
  256.3 3.1 fusion.78
  259.4 8.7 %fusion.13 = (bf16[256,512]{0,1:T(8,128)(2,1)S(1)}, bf16[256,512]{0,1:T(8,128)(2,1)S(1)}) fusion(f32[16,512]{1,0:T(8,128)S(1)} %get-tuple-element.46, f32[16,512]{1,0:T(8,128)S(1)} %get-tuple-element.48, f32[512,256,16]{1,0,2:T(8,128)S(1)} %fusion.76, f32[512,256,16]{1,0,2:T(8,128)S(1)} %fusion.78, f32[512,256,16]{1,0,2:T(8,128)S(1)} %fusion.94, ...), kind=kOutput, calls=%fused_computation.27 | convolution fusion | flops 1096548352 | bytes 27854848 | tf_op jit(solution)/shard_map/osi,ik->sok/dot_general | solution.py:41
  268.1 0.8 pad_maximum_fusion.3
  269.2 57.9 %all-gather.6.cloned.1.call-done = bf16[2,4096,512]{1,2,0:T(8,128)(2,1)} async-done(((bf16[2,256,512]{1,2,0:T(8,128)(2,1)}), bf16[2,4096,512]{1,2,0:T(8,128)(2,1)}) %all-gather.6.cloned.1.call-update) | async-done | bytes 8388624 | tf_op jit(solution)/shard_map/all_gather | solution.py:98
  327.1 5.9 %fusion.316 = (bf16[1,4096,512]{1,2,0:T(8,128)(2,1)}, bf16[1,4096,512]{1,2,0:T(8,128)(2,1)}) fusion(bf16[2,4096,512]{1,2,0:T(8,128)(2,1)} %all-gather.6.cloned.1.call-done), kind=kLoop, calls=%fused_computation.399 | loop fusion | bytes 16777216 | tf_op jit(solution)/shard_map/slice | solution.py:43
  333.0 6.5 %copy.51 = bf16[1,4096,512]{2,1,0:T(8,128)(2,1)} copy(bf16[1,4096,512]{1,2,0:T(8,128)(2,1)} %get-tuple-element.22) | data formatting | bytes 8388608 | tf_op jit(solution)/shard_map/slice | solution.py:43
  339.5 7.8 %fusion.105 = f32[256,16,512]{2,0,1:T(8,128)} fusion(bf16[16,256,512]{2,1,0:T(8,128)(2,1)} %bitcast.399, s32[256]{0:T(256)S(1)} %iota_add_fusion.1), kind=kOutput, calls=%fused_computation.169 | convolution fusion | flops 1074790400 | bytes 12583936 | tf_op jit(solution)/shard_map/sio,ik->sko/dot_general | solution.py:41
  347.3 5.5 fusion.123
  352.8 6.5 %copy.50 = bf16[1,4096,512]{2,1,0:T(8,128)(2,1)} copy(bf16[1,4096,512]{1,2,0:T(8,128)(2,1)} %get-tuple-element.23) | data formatting | bytes 8388608 | tf_op jit(solution)/shard_map/slice | solution.py:43
  359.2 4.6 fusion.107
  363.8 1.3 copy-done.2
  365.1 8.0 %fusion.9 = (bf16[256,512]{1,0:T(8,128)(2,1)S(1)}, bf16[256,512]{1,0:T(8,128)(2,1)S(1)}) fusion(f32[16,256]{1,0:T(8,128)S(1)} %get-tuple-element.49, f32[16,256]{1,0:T(8,128)S(1)} %get-tuple-element.51, f32[256,16,512]{2,0,1:T(8,128)} %fusion.105, f32[256,16,512]{2,0,1:T(8,128)S(1)} %fusion.107, f32[256,16,512]{2,0,1:T(8,128)S(1)} %copy-done.2, ...), kind=kOutput, calls=%fused_computation.19 | convolution fusion | flops 1095499776 | bytes 29918208 | tf_op jit(solution)/shard_map/sio,ik->sko/dot_general | solution.py:41
  373.2 1.3 collective-permute-start.3
  374.5 4.0 collective-permute-start.2
  380.9 1.3 pad_maximum_fusion
  382.2 0.3 constant_dynamic-slice_fusion.4
  384.6 2.1 fusion.53
  386.7 0.8 pad_maximum_fusion.5
  387.6 57.9 %all-gather.8.cloned.1.call-done = bf16[2,4096,512]{2,1,0:T(8,128)(2,1)} async-done(((bf16[2,256,512]{2,1,0:T(8,128)(2,1)}), bf16[2,4096,512]{2,1,0:T(8,128)(2,1)}) %all-gather.8.cloned.1.call-update) | async-done | bytes 8388624 | tf_op jit(solution)/shard_map/all_gather | solution.py:98
  445.5 3.8 fusion.315
  449.3 2.2 fusion.101
  451.5 2.3 fusion.115
  453.7 2.2 fusion.103
  456.0 6.4 %fusion.5 = (bf16[256,512]{1,0:T(8,128)(2,1)S(1)}, bf16[256,512]{1,0:T(8,128)(2,1)S(1)}) fusion(f32[16,256]{1,0:T(8,128)S(1)} %get-tuple-element.50, f32[16,256]{1,0:T(8,128)S(1)} %get-tuple-element.51, f32[256,16,512]{2,0,1:T(8,128)S(1)} %fusion.101, f32[256,16,512]{2,0,1:T(8,128)S(1)} %fusion.103, f32[256,16,512]{2,0,1:T(8,128)S(1)} %fusion.115, ...), kind=kOutput, calls=%fused_computation.11 | convolution fusion | flops 1095499776 | bytes 29918208 | tf_op jit(solution)/shard_map/sio,ik->sko/dot_general | solution.py:41
  462.6 0.4 stack.124
  463.0 58.1 %all_to_all.16 = bf16[8,2,256,512]{2,3,1,0:T(8,128)(2,1)S(1)} all-to-all(bf16[8,2,256,512]{2,3,1,0:T(8,128)(2,1)S(1)} %stack.124), channel_id=1, replica_groups=mesh['rows'=16,'cols'=8] {'cols'}, dimensions={0} | all-to-all | bytes 8388608 | tf_op jit(solution)/shard_map/all_to_all | solution.py:105
  521.1 0.4 copy.80
  521.5 0.4 fusion.318
  521.9 3.1 fusion.72
  525.0 3.2 fusion.86
  528.2 3.1 fusion.74
  531.3 8.7 %fusion.1 = (f32[256,512]{0,1:T(8,128)S(1)}, f32[256,512]{0,1:T(8,128)S(1)}) fusion(f32[16,512]{1,0:T(8,128)S(1)} %get-tuple-element.47, f32[16,512]{1,0:T(8,128)S(1)} %get-tuple-element.48, f32[512,256,16]{1,0,2:T(8,128)S(1)} %fusion.72, f32[512,256,16]{1,0,2:T(8,128)S(1)} %fusion.74, f32[512,256,16]{1,0,2:T(8,128)S(1)} %fusion.86, ...), kind=kOutput, calls=%fused_computation.3 | convolution fusion | flops 1096548352 | bytes 28379136 | tf_op jit(solution)/shard_map/osi,ik->sok/dot_general | solution.py:41
  540.1 1.3 copy.58
  (62 shorter events, 7.1 us)
Async XLA Ops:
  6.5 11.5 %copy-start.4 = (bf16[2,256,512]{2,1,0:T(8,128)(2,1)S(1)}, bf16[2,256,512]{2,1,0:T(8,128)(2,1)}, u32[]{:S(2)}) copy-start(bf16[2,256,512]{2,1,0:T(8,128)(2,1)} %param.6) | copy-start | bytes 1572868
  6.5 11.2 %copy-start.3 = (bf16[2,2,3,128,128]{4,3,2,1,0:T(8,128)(2,1)S(1)}, bf16[2,2,3,128,128]{4,3,2,1,0:T(8,128)(2,1)}, u32[]{:S(2)}) copy-start(bf16[2,2,3,128,128]{4,3,2,1,0:T(8,128)(2,1)} %param.7) | copy-start | bytes 1179652
  6.5 75.5 %all-gather.4.cloned.1.call-start = ((), (), s32[]{:S(2)}) async-start(), calls=%async_computation.3 | async-start | bytes 8912896 | tf_op jit(solution)/shard_map/all_gather | solution.py:98
  6.5 11.4 %collective-permute-start = (bf16[2,256,512]{2,1,0:T(8,128)(2,1)}, bf16[2,256,512]{2,1,0:T(8,128)(2,1)S(1)}, u32[]{:S(2)}, u32[]{:S(2)}) collective-permute-start(bf16[2,256,512]{2,1,0:T(8,128)(2,1)} %param.6), channel_id=1, source_target_pairs={{0,8},{8,16},{16,24},{24,32},{32,40},{40,48},{48,56},{56,64},{64,7... | collective-permute-start | bytes 1572872 | tf_op jit(solution)/shard_map/ppermute | solution.py:15
  8.0 10.1 %collective-permute-start.1 = (bf16[2,256,512]{2,1,0:T(8,128)(2,1)}, bf16[2,256,512]{2,1,0:T(8,128)(2,1)S(1)}, u32[]{:S(2)}, u32[]{:S(2)}) collective-permute-start(bf16[2,256,512]{2,1,0:T(8,128)(2,1)} %param.6), channel_id=1, source_target_pairs={{8,0},{16,8},{24,16},{32,24},{40,32},{48,40},{56,48},{64,56},{72,6... | collective-permute-start | bytes 1572872 | tf_op jit(solution)/shard_map/ppermute | solution.py:15
  19.0 1.2 copy-start.5
  101.6 7.1 %copy-start.6 = (f32[256,512]{1,0:T(8,128)S(1)}, f32[256,512]{1,0:T(8,128)}, u32[]{:S(2)}) copy-start(f32[256,512]{1,0:T(8,128)} %param.10) | copy-start | bytes 1572868
  101.6 58.2 %all-to-all-start = ((bf16[8,2,256,512]{2,3,1,0:T(8,128)(2,1)}), bf16[8,2,256,512]{2,3,1,0:T(8,128)(2,1)}, u32[]{:S(2)}, u32[]{:S(2)}) async-start(bf16[8,2,256,512]{2,3,1,0:T(8,128)(2,1)} %stack.109), calls=%async_computation | async-start | bytes 8388608 | tf_op jit(solution)/shard_map/all_to_all | solution.py:105
  108.4 218.7 %all-gather.6.cloned.1.call-start = ((), (), s32[]{:S(2)}) async-start(), calls=%async_computation.4 | async-start | bytes 8912896 | tf_op jit(solution)/shard_map/all_gather | solution.py:98
  269.0 176.5 %all-gather.8.cloned.1.call-start = ((), (), s32[]{:S(2)}) async-start(), calls=%async_computation.5 | async-start | bytes 8912896 | tf_op jit(solution)/shard_map/all_gather | solution.py:98
  339.5 7.8 %copy-start = (bf16[1,4096,512]{2,1,0:T(8,128)(2,1)S(1)}, bf16[1,4096,512]{2,1,0:T(8,128)(2,1)}, u32[]{:S(2)}) copy-start(bf16[1,4096,512]{2,1,0:T(8,128)(2,1)} %copy.51) | copy-start | bytes 12582916
  359.2 4.6 copy-start.1
  359.2 5.9 %copy-start.2 = (f32[256,16,512]{2,0,1:T(8,128)S(1)}, f32[256,16,512]{2,0,1:T(8,128)}, u32[]{:S(2)}) copy-start(f32[256,16,512]{2,0,1:T(8,128)} %fusion.123) | copy-start | bytes 25165828
  373.2 7.7 %collective-permute-start.3 = (bf16[2,256,512]{2,1,0:T(8,128)(2,1)S(1)}, bf16[2,256,512]{2,1,0:T(8,128)(2,1)}, u32[]{:S(2)}, u32[]{:S(2)}) collective-permute-start(bf16[2,256,512]{2,1,0:T(8,128)(2,1)S(1)} %pad_maximum_fusion.4), channel_id=1, source_target_pairs={{8,0},{16,8},{24,16},{32,24},{40,32},{48,40},{56,48},{64,56},{72,6... | collective-permute-start | bytes 1572872 | tf_op jit(solution)/shard_map/ppermute | solution.py:15
  374.5 6.4 %collective-permute-start.2 = (bf16[2,256,512]{2,1,0:T(8,128)(2,1)S(1)}, bf16[2,256,512]{2,1,0:T(8,128)(2,1)}, u32[]{:S(2)}, u32[]{:S(2)}) collective-permute-start(bf16[2,256,512]{2,1,0:T(8,128)(2,1)S(1)} %pad_maximum_fusion.4), channel_id=1, source_target_pairs={{0,8},{8,16},{16,24},{24,32},{32,40},{40,48},{48,56},{56,64},{64,7... | collective-permute-start | bytes 1572872 | tf_op jit(solution)/shard_map/ppermute | solution.py:15
Sparse Core Ops, SparseCore 0:
  23.2 58.7 all-gather.3
  269.1 57.9 all-gather.5
  387.7 57.7 all-gather.7
